TPU v7x, 256 devices: a whole 4x4x8 slice. The times are simulated.
256 devices in a mesh: mem: 16 (over y, x), reg: 16 (over z, core).
Axes of the slice: x: 4, y: 4, z: 8, core: 2. Of those that a mesh axis runs over, the one named last changes fastest.
Arguments:
- prior_states: bfloat16 [256, 227, 8192], P('mem', None, 'reg'), may hold values from -6 to 6
- sensor_space_runs: bfloat16 [256, 16, 8192], P('mem', 'reg'), may hold values from -6 to 6
- sensor_readings: float32 [16, 8192], P('reg'), may hold values from -8 to 8
- noise_precision: float32 [16, 8192], P('reg'), may hold values from 0.1 to 1
- reading_pointers: int32 [16, 16, 4, 512], P('reg', 'mem'), may hold values from 0 to 8703, as said below
- reading_tally: int32 [16, 16, 4], P('reg', 'mem'), may hold values from 128 to 512, as said below
Outputs:
- analysis: bfloat16 [256, 227, 8192], P('mem', None, 'reg')
Inputs may be any that keep to these rules, and one draw needn't show every extreme that they name: Row reading_pointers[r, m, g, :] holds 512 distinct positions of region r's extended observations, together one window of 512 consecutive positions, in an order drawn from the seed. A local analysis uses the first reading_tally[r, m, g] entries of its list.
All inputs are finite; a program needn't handle non-finite values.
Results may differ from a plain program's by a relative error of at most 0.009.
Values may be sent and summed in bfloat16 or wider, within the bound.
No kernel may reach another device: no remote copies, remote signals or barrier semaphores. Data moves between devices by JAX's collectives and lax.ppermute only.
A program may use at most 128 MiB of HBM per device.

v0:
```python
import math
import jax
import jax.numpy as jnp
from jax import lax
from jax.sharding import PartitionSpec as P

NS_ITERS = 6
HW = 256
inflation = 1.1
highest = lax.Precision.HIGHEST


def with_halo(cells, sides, width):
    for axis, dim in sides:
        count = lax.axis_size(axis)
        head = lax.slice_in_dim(cells, 0, width, axis=dim)
        tail = lax.slice_in_dim(cells, cells.shape[dim] - width, cells.shape[dim], axis=dim)
        cells = jnp.concatenate(
            [
                lax.ppermute(tail, axis, [(i, (i + 1) % count) for i in range(count)]),
                cells,
                lax.ppermute(head, axis, [((i + 1) % count, i) for i in range(count)]),
            ],
            axis=dim,
        )
    return cells


def nearby_correction(
    prior_patch, sensor_space_lines, sensor_readings, precision_nearby, pending_amount
):
    runs_sequence = prior_patch.shape[0]
    prior_states_narrow = prior_patch.astype(jnp.float32)
    middle_pillar = jnp.mean(prior_states_narrow, axis=0)
    deviation_matrix = (prior_states_narrow - middle_pillar[None]).astype(jnp.bfloat16)
    observed_f32 = sensor_space_lines.astype(jnp.float32)
    ens_mean = jnp.mean(observed_f32, axis=0)
    anomaly = lax.optimization_barrier((observed_f32 - ens_mean[None]).astype(jnp.bfloat16)).astype(
        jnp.float32
    )
    active = (jnp.arange(sensor_space_lines.shape[1], dtype=jnp.int32) < pending_amount).astype(
        jnp.float32
    )
    weight = precision_nearby * active
    identity = jnp.eye(runs_sequence, dtype=jnp.float32)
    gram_matrix = (
        jnp.dot(anomaly, (anomaly * weight[None, :]).T, precision=highest)
        + (runs_sequence - 1) / inflation * identity
    )
    innovation_sum = jnp.dot(anomaly, weight * (sensor_readings - ens_mean), precision=highest)
    frobenius = jnp.sqrt(jnp.sum(gram_matrix * gram_matrix))
    iterate = gram_matrix / frobenius
    inverse_root = identity
    for iteration in range(NS_ITERS):
        factor = 1.5 * identity - 0.5 * jnp.dot(inverse_root, iterate, precision=highest)
        iterate = jnp.dot(iterate, factor, precision=highest)
        inverse_root = jnp.dot(factor, inverse_root, precision=highest)
    inverse_root = inverse_root / jnp.sqrt(frobenius)
    mean_weight = jnp.dot(
        inverse_root, jnp.dot(inverse_root, innovation_sum, precision=highest), precision=highest
    )
    transform = (math.sqrt(runs_sequence - 1) * inverse_root + mean_weight[:, None]).astype(
        jnp.bfloat16
    )
    combined = jnp.einsum(
        "jvc,jk->kvc",
        deviation_matrix.astype(jnp.float32),
        transform.astype(jnp.float32),
        precision=highest,
    )
    return (middle_pillar[None] + combined).astype(jnp.bfloat16)


def per_device(
    prior_states,
    sensor_space_runs,
    sensor_readings,
    noise_precision,
    reading_pointers,
    reading_tally,
):
    pillar_sequence = lax.all_to_all(prior_states, "mem", split_axis=2, concat_axis=0, tiled=True)
    runs_sequence, fields_sequence, columns_here = pillar_sequence.shape
    patch_amount = reading_tally.shape[2]
    patch_width = columns_here // patch_amount
    extended = with_halo(sensor_space_runs, (("reg", 2),), HW)
    statistics = jnp.stack([sensor_readings, noise_precision])
    stats_extended = with_halo(statistics.astype(jnp.bfloat16), (("reg", 2),), HW).astype(
        statistics.dtype
    )
    own_lists = reading_pointers[0, 0]
    gathered = lax.all_gather(extended, "mem", axis=0, tiled=True)
    sensor_space_lines = jnp.take(gathered[:, 0], own_lists.reshape(-1), axis=1)
    sensor_space_lines = sensor_space_lines.reshape(runs_sequence, patch_amount, -1)
    chosen_moments = jnp.take(stats_extended[:, 0], own_lists, axis=1)
    prior_patches = pillar_sequence.reshape(
        runs_sequence, fields_sequence, patch_amount, patch_width
    )
    analysed = jax.vmap(nearby_correction, in_axes=(2, 1, 0, 0, 0), out_axes=2)(
        prior_patches, sensor_space_lines, chosen_moments[0], chosen_moments[1], reading_tally[0, 0]
    )
    analysed = analysed.reshape(runs_sequence, fields_sequence, columns_here)
    return lax.all_to_all(analysed, "mem", split_axis=0, concat_axis=2, tiled=True)


def solution(mesh):
    placed = (
        P("mem", None, "reg"),
        P("mem", "reg", None),
        P("reg", None),
        P("reg", None),
        P("reg", "mem", None, None),
        P("reg", "mem", None),
    )
    return jax.shard_map(
        per_device, mesh=mesh, in_specs=placed, out_specs=P("mem", None, "reg"), check_vma=False
    )
```

profile of v0, /device:TPU:96, one launch (start us, length us, event | category | flops | bytes accessed | tf_op | source)
XLA Modules:
  0.0 244.3 jit_solution(5536810041124589090)
XLA Ops:
  8.6 1.7 collective-permute-done
  10.3 1.7 pad_maximum_fusion
  12.0 8.4 %copy.29 = bf16[16,227,512]{1,0,2:T(8,128)(2,1)} copy(bf16[16,227,512]{2,0,1:T(8,128)(2,1)} %param.6) | data formatting | bytes 7438336 | tf_op args[0]
  20.4 7.2 %all-to-all-start = ((bf16[16,227,512]{1,0,2:T(8,128)(2,1)}), bf16[16,227,512]{1,0,2:T(8,128)(2,1)}, u32[]{:S(2)}, u32[]{:S(2)}) async-start(bf16[16,227,512]{1,0,2:T(8,128)(2,1)} %copy.29), calls=%async_computation | async-start | bytes 8388608 | tf_op jit(solution)/shard_map/all_to_all | solution.py:82
  27.8 1.2 collective-permute-start.2
  30.9 2.8 %copy.33 = f32[2,8704]{0,1:T(8,128)} copy(f32[2,8704]{1,0:T(2,128)S(1)} %maximum_convert_fusion) | data formatting | bytes 139264 | tf_op jit(solution)/shard_map/convert_element_type | solution.py:88
  33.6 7.7 %gather_fusion.1 = f32[2048,2]{1,0:T(8,128)S(1)} fusion(f32[2,8704]{0,1:T(8,128)} %copy.33, s32[2048]{0:T(1024)S(1)} %broadcast_clamp_fusion), kind=kCustom, calls=%fused_computation.1 | custom fusion | bytes 40960 | tf_op jit(solution)/shard_map/jit(_take)/gather | solution.py:95
  41.7 57.3 %all-to-all-done = bf16[16,227,512]{1,0,2:T(8,128)(2,1)} async-done(((bf16[16,227,512]{1,0,2:T(8,128)(2,1)}), bf16[16,227,512]{1,0,2:T(8,128)(2,1)}, u32[]{:S(2)}, u32[]{:S(2)}) %all-to-all-start) | async-done | bytes 3719200 | tf_op jit(solution)/shard_map/all_to_all | solution.py:82
  99.0 3.6 %copy_convert_fusion = f32[16,227,512]{1,2,0:T(8,128)S(1)} fusion(bf16[16,227,512]{1,0,2:T(8,128)(2,1)} %all-to-all-done), kind=kLoop, calls=%fused_computation.7 | loop fusion | flops 1859584 | bytes 11157504 | tf_op jit(solution)/shard_map/vmap()/convert_element_type | solution.py:33
  102.6 4.1 %copy.35 = f32[16,16,227,32]{2,3,1,0:T(8,128)} copy(f32[16,16,227,32]{2,3,0,1:T(8,128)S(1)} %bitcast.130) | data formatting | bytes 14876672 | tf_op jit(solution)/shard_map/vmap()/transpose | solution.py:35
  106.7 3.7 %fusion.8 = f32[227,512]{0,1:T(8,128)S(1)} fusion(bf16[16,227,512]{1,0,2:T(8,128)(2,1)} %all-to-all-done), kind=kLoop, calls=%fused_computation.13 | loop fusion | flops 3602944 | bytes 4184064 | tf_op jit(solution)/shard_map/vmap()/reduce_sum | solution.py:34
  110.5 6.7 %subtract_convert_fusion = bf16[4,256,227,8]{2,3,0,1:T(8,128)(2,1)} fusion(f32[4,256,227,8]{2,3,0,1:T(8,128)} %bitcast.129, f32[4,227,8]{1,2,0:T(8,128)S(1)} %get-tuple-element.15), kind=kLoop, calls=%fused_computation.2 | loop fusion | flops 3719168 | bytes 11186560 | tf_op jit(solution)/shard_map/vmap()/convert_element_type | solution.py:35
  117.2 6.6 %copy.31 = bf16[256,1,8704]{0,2,1:T(8,128)(2,1)} copy(bf16[256,1,8704]{2,0,1:T(8,128)(2,1)} %all-gather.2.cloned.1.call-done) | data formatting | bytes 8912896 | tf_op jit(solution)/shard_map/all_gather | solution.py:92
  123.8 9.5 %gather_fusion = bf16[2048,256]{1,0:T(8,128)(2,1)S(1)} fusion(bf16[256,8704]{0,1:T(8,128)(2,1)} %bitcast.128, s32[2048]{0:T(1024)S(1)} %broadcast_clamp_fusion.1), kind=kCustom, calls=%fused_computation | custom fusion | bytes 2105344 | tf_op jit(solution)/shard_map/jit(_take)/gather | solution.py:93
  135.2 1.5 multiply_reduce_fusion
  138.1 1.2 fusion.31
  139.3 1.2 fusion.16
  146.4 1.4 fusion.14
  154.5 1.2 fusion.12
  158.9 5.6 %fusion = bf16[256,227,4,8]{0,1,3,2:T(8,128)(2,1)} fusion(f32[227,4,8]{0,2,1:T(8,128)S(1)} %get-tuple-element.16, bf16[4,256,227,8]{2,3,0,1:T(8,128)(2,1)S(1)} %copy-done, f32[4,256,256]{2,1,0:T(8,128)S(1)} %convolution_divide_fusion, f32[4,256]{1,0:T(4,128)S(1)} %bitcast.144), kind=kOutput, calls=%fused_computation.4 | convolution fusion | flops 956612608 | bytes 8520064 | tf_op jit(solution)/shard_map/vmap(jvc,jk->kvc)/dot_general | solution.py:65
  164.5 7.8 %copy.37 = bf16[256,227,32]{1,2,0:T(8,128)(2,1)} copy(bf16[256,227,32]{0,1,2:T(8,128)(2,1)} %bitcast.134) | data formatting | bytes 7438336 | tf_op jit(solution)/shard_map/reshape | solution.py:102
  172.3 55.4 %all_to_all.27 = bf16[256,227,32]{1,2,0:T(8,128)(2,1)S(1)} all-to-all(bf16[256,227,32]{1,2,0:T(8,128)(2,1)} %copy.37), channel_id=1, replica_groups=mesh['mem'=16,'reg'=16] {'mem'}, dimensions={0} | all-to-all | bytes 7438336 | tf_op jit(solution)/shard_map/all_to_all | solution.py:103
  227.8 2.4 copy.38
  230.2 7.3 %copy.39 = bf16[16,227,512]{2,0,1:T(8,128)(2,1)} copy(bf16[16,227,512]{1,2,0:T(8,128)(2,1)} %bitcast.132) | data formatting | bytes 7438336 | tf_op jit(solution)/shard_map/all_to_all | solution.py:103
  (64 shorter events, 23.3 us)
Async XLA Ops:
  6.5 110.7 %all-gather.2.cloned.1.call-start = ((), (), s32[]{:S(2)}) async-start(), calls=%async_computation.2 | async-start | bytes 4734976 | tf_op jit(solution)/shard_map/all_gather | solution.py:92
  7.3 1.4 collective-permute-start.1
  7.3 3.1 %collective-permute-start = (bf16[16,1,256]{2,0,1:T(8,128)(2,1)S(1)}, bf16[16,1,256]{2,0,1:T(8,128)(2,1)S(1)}, u32[]{:S(2)}, u32[]{:S(2)}) collective-permute-start(bf16[16,1,256]{2,0,1:T(8,128)(2,1)S(1)} %get-tuple-element.7), channel_id=1, source_target_pairs={{0,1},{1,2},{2,3},{3,4},{4,5},{5,6},{6,7},{7,8},{8,9},{9,10},{10,1... | collective-permute-start | bytes 24584 | tf_op jit(solution)/shard_map/ppermute | solution.py:20
  20.4 7.2 %copy-start.2 = (f32[1,8192]{1,0:T(1,128)S(1)}, f32[1,8192]{1,0:T(1,128)}, u32[]{:S(2)}) copy-start(f32[1,8192]{1,0:T(1,128)} %param.8) | copy-start | bytes 98308
  20.4 7.2 %copy-start.3 = (f32[1,8192]{1,0:T(1,128)S(1)}, f32[1,8192]{1,0:T(1,128)}, u32[]{:S(2)}) copy-start(f32[1,8192]{1,0:T(1,128)} %param.9) | copy-start | bytes 98308
  20.4 8.6 %copy-start.1 = (s32[1,1,4,512]{3,2,1,0:T(4,128)S(1)}, s32[1,1,4,512]{3,2,1,0:T(4,128)}, u32[]{:S(2)}) copy-start(s32[1,1,4,512]{3,2,1,0:T(4,128)} %param.10) | copy-start | bytes 24580
  20.4 78.6 %all-to-all-start = ((bf16[16,227,512]{1,0,2:T(8,128)(2,1)}), bf16[16,227,512]{1,0,2:T(8,128)(2,1)}, u32[]{:S(2)}, u32[]{:S(2)}) async-start(bf16[16,227,512]{1,0,2:T(8,128)(2,1)} %copy.29), calls=%async_computation | async-start | bytes 8388608 | tf_op jit(solution)/shard_map/all_to_all | solution.py:82
  27.8 1.9 collective-permute-start.3
  27.8 3.0 %collective-permute-start.2 = (bf16[2,1,256]{2,0,1:T(2,128)(2,1)S(1)}, bf16[2,1,256]{2,0,1:T(2,128)(2,1)S(1)}, u32[]{:S(2)}, u32[]{:S(2)}) collective-permute-start(bf16[2,1,256]{2,0,1:T(2,128)(2,1)S(1)} %get-tuple-element.9), channel_id=1, source_target_pairs={{0,1},{1,2},{2,3},{3,4},{4,5},{5,6},{6,7},{7,8},{8,9},{9,10},{10,1... | collective-permute-start | bytes 3080 | tf_op jit(solution)/shard_map/ppermute | solution.py:20
  133.3 1.8 copy-start.4
  154.5 4.4 %copy-start = (bf16[4,256,227,8]{2,3,0,1:T(8,128)(2,1)S(1)}, bf16[4,256,227,8]{2,3,0,1:T(8,128)(2,1)}, u32[]{:S(2)}) copy-start(bf16[4,256,227,8]{2,3,0,1:T(8,128)(2,1)} %subtract_convert_fusion) | copy-start | bytes 11157508
Sparse Core Ops, SparseCore 0:
  12.2 104.1 all-gather.1
where the time goes:
time: 245 us; the launch traced here: 244 us
  waiting for transfers between devices  61.4 us (25%)
  local copies, waits for them, and re-layouts  58.5 us (24%)
  blocking collectives  55.4 us (23%)
  matrix products  29.2 us (12%)
  other arithmetic  17.1 us (7%)
  between operations  13.8 us (6%)
  starting transfers between devices  8.99 us (4%)
    all_to_all x1, waiting for transfers between devices, per_device(): lax.all_to_all(prior_states, 'mem', split_axis=2, concat_axis=0, tiled=True)  57.3 us
    all_to_all x1, blocking collectives, per_device(): lax.all_to_all(analysed, 'mem', split_axis=0, concat_axis=2, tiled=True)  55.4 us
    gather x2, local copies, waits for them, and re-layouts, per_device(): sensor_space_lines = jnp.take(gathered[:, 0], own_lists.reshape(-1), axis=1)  10.2 us
    all_to_all x2, local copies, waits for them, and re-layouts, per_device(): lax.all_to_all(analysed, 'mem', split_axis=0, concat_axis=2, tiled=True)  9.72 us
    unnamed x14, local copies, waits for them, and re-layouts  8.41 us
    gather x2, local copies, waits for them, and re-layouts, per_device(): chosen_moments = jnp.take(stats_extended[:, 0], own_lists, axis=1)  8.07 us
    reshape x1, local copies, waits for them, and re-layouts, per_device(): analysed = analysed.reshape(runs_sequence, fields_sequence, columns_here)  7.84 us
    all_to_all x1, starting transfers between devices, per_device(): lax.all_to_all(prior_states, 'mem', split_axis=2, concat_axis=0, tiled=True)  7.22 us
  transfers between devices with their start and end apart: 6, of which 5 were waited for; matrix products, arithmetic and copies ran while one was open for 15% of the time, Pallas kernels for 0%

commit v1 on v0

--- a/solution.py
+++ b/solution.py
@@ -8,6 +8,12 @@
 HW = 256
 inflation = 1.1
 highest = lax.Precision.HIGHEST
+refer_surface = lambda mine_x, comm_axis, dim_k: jnp.concatenate(
+    lax.all_to_all(
+        jnp.stack([mine_x for _ in range(lax.psum(1, comm_axis))], axis=0), comm_axis, 0, 0
+    ),
+    axis=dim_k,
+)
 
 
 def with_halo(cells, sides, width):
@@ -89,7 +95,7 @@
         statistics.dtype
     )
     own_lists = reading_pointers[0, 0]
-    gathered = lax.all_gather(extended, "mem", axis=0, tiled=True)
+    gathered = refer_surface(extended, "mem", 0)
     sensor_space_lines = jnp.take(gathered[:, 0], own_lists.reshape(-1), axis=1)
     sensor_space_lines = sensor_space_lines.reshape(runs_sequence, patch_amount, -1)
     chosen_moments = jnp.take(stats_extended[:, 0], own_lists, axis=1)

time: 245 us -> 270 us (1.10)
  waiting for transfers between devices: 61.4 us -> 95.2 us
  between operations: 13.8 us -> 0.41 us
  starting transfers between devices: 8.99 us -> 15.3 us
    all_to_all x0 -> x1, waiting for transfers between devices: none -> 35.4 us  [lax.all_to_all(jnp.stack([mine_x for _ in range(lax.psum(1, comm_axis))],...]
    another operation x0 -> x2, local copies, waits for them, and re-layouts: none -> 9.03 us  [the longest x1 6.58 us: per_device(): sensor_space_lines = jnp.take(gathered[:, 0], own_lists.reshape(-1), axis=1)]
    all_gather x1 -> x0, local copies, waits for them, and re-layouts: 6.61 us -> none  [per_device(): gathered = lax.all_gather(extended, 'mem', axis=0, tiled=True)]
    all_to_all x0 -> x1, starting transfers between devices: none -> 4.71 us  [lax.all_to_all(jnp.stack([mine_x for _ in range(lax.psum(1, comm_axis))],...]
    ppermute x2, waiting for transfers between devices: 2.86 us -> 0.01 us  [with_halo(): lax.ppermute(tail, axis, [(i, (i + 1) % count) for i in range(count)])]
    unnamed x14 -> x16, local copies, waits for them, and re-layouts: 8.41 us -> 8.28 us
  transfers between devices with their start and end apart: 6 -> 6, of which waited for: 5 -> 2; matrix products, arithmetic and copies ran while one was open for 15% -> 12% of each run, Pallas kernels for 0% -> 0%
where the time goes in v1:
time: 270 us; the launch traced here: 269 us
  waiting for transfers between devices  95.2 us (35%)
  local copies, waits for them, and re-layouts  60 us (22%)
  blocking collectives  53.6 us (20%)
  matrix products  29.2 us (11%)
  starting transfers between devices  15.3 us (6%)
  other arithmetic  15.2 us (6%)
    all_to_all x1, waiting for transfers between devices, per_device(): lax.all_to_all(prior_states, 'mem', split_axis=2, concat_axis=0, tiled=True)  59.8 us
    all_to_all x1, blocking collectives, per_device(): lax.all_to_all(analysed, 'mem', split_axis=0, concat_axis=2, tiled=True)  53.6 us
    all_to_all x1, waiting for transfers between devices, lax.all_to_all(jnp.stack([mine_x for _ in range(lax.psum(1, comm_axis))],...  35.4 us
    gather x2, local copies, waits for them, and re-layouts, per_device(): sensor_space_lines = jnp.take(gathered[:, 0], own_lists.reshape(-1), axis=1)  10.2 us
    all_to_all x2, local copies, waits for them, and re-layouts, per_device(): lax.all_to_all(analysed, 'mem', split_axis=0, concat_axis=2, tiled=True)  9.72 us
    unnamed x16, local copies, waits for them, and re-layouts  8.28 us
    gather x2, local copies, waits for them, and re-layouts, per_device(): chosen_moments = jnp.take(stats_extended[:, 0], own_lists, axis=1)  8.05 us
    reshape x1, local copies, waits for them, and re-layouts, per_device(): analysed = analysed.reshape(runs_sequence, fields_sequence, columns_here)  7.84 us
  transfers between devices with their start and end apart: 6, of which 2 were waited for; matrix products, arithmetic and copies ran while one was open for 12% of the time, Pallas kernels for 0%

profile of v1, /device:TPU:96, one launch (start us, length us, event | category | flops | bytes accessed | tf_op | source)
XLA Modules:
  0.0 268.8 jit_solution(1916497707100479624)
XLA Ops:
  0.0 8.2 %copy.25 = bf16[16,227,512]{1,0,2:T(8,128)(2,1)} copy(bf16[16,227,512]{2,0,1:T(8,128)(2,1)} %param.6) | data formatting | bytes 7438336 | tf_op args[0]
  8.2 7.2 %all-to-all-start = ((bf16[16,227,512]{1,0,2:T(8,128)(2,1)}), bf16[16,227,512]{1,0,2:T(8,128)(2,1)}, u32[]{:S(2)}, u32[]{:S(2)}) async-start(bf16[16,227,512]{1,0,2:T(8,128)(2,1)} %copy.25), calls=%async_computation | async-start | bytes 8388608 | tf_op jit(solution)/shard_map/all_to_all | solution.py:88
  16.1 1.3 collective-permute-start.3
  17.4 1.5 collective-permute-start.2
  19.0 59.8 %all-to-all-done = bf16[16,227,512]{1,0,2:T(8,128)(2,1)} async-done(((bf16[16,227,512]{1,0,2:T(8,128)(2,1)}), bf16[16,227,512]{1,0,2:T(8,128)(2,1)}, u32[]{:S(2)}, u32[]{:S(2)}) %all-to-all-start) | async-done | bytes 3719200 | tf_op jit(solution)/shard_map/all_to_all | solution.py:88
  78.8 2.4 stack.10
  81.2 4.7 %all-to-all-start.1 = ((bf16[16,16,1,8704]{3,1,2,0:T(8,128)(2,1)}), bf16[16,16,1,8704]{3,1,2,0:T(8,128)(2,1)}, u32[]{:S(2)}, u32[]{:S(2)}) async-start(bf16[16,16,1,8704]{3,1,2,0:T(8,128)(2,1)} %stack.10), calls=%async_computation.1 | async-start | bytes 8912896 | tf_op jit(solution)/shard_map/all_to_all | solution.py:12
  86.2 2.7 %copy.29 = f32[2,8704]{0,1:T(8,128)} copy(f32[2,8704]{1,0:T(2,128)S(1)} %maximum_convert_fusion) | data formatting | bytes 139264 | tf_op jit(solution)/shard_map/convert_element_type | solution.py:94
  88.9 7.7 %gather_fusion.1 = f32[2048,2]{1,0:T(8,128)S(1)} fusion(f32[2,8704]{0,1:T(8,128)} %copy.29, s32[2048]{0:T(1024)S(1)} %broadcast_clamp_fusion), kind=kCustom, calls=%fused_computation.1 | custom fusion | bytes 40960 | tf_op jit(solution)/shard_map/jit(_take)/gather | solution.py:101
  97.0 3.5 %copy_convert_fusion = f32[16,227,512]{1,2,0:T(8,128)S(1)} fusion(bf16[16,227,512]{1,0,2:T(8,128)(2,1)} %all-to-all-done), kind=kLoop, calls=%fused_computation.7 | loop fusion | flops 1859584 | bytes 11157504 | tf_op jit(solution)/shard_map/vmap()/convert_element_type | solution.py:39
  100.6 4.1 %copy.31 = f32[16,16,227,32]{2,3,1,0:T(8,128)} copy(f32[16,16,227,32]{2,3,0,1:T(8,128)S(1)} %bitcast.131) | data formatting | bytes 14876672 | tf_op jit(solution)/shard_map/vmap()/transpose | solution.py:41
  104.7 3.6 %fusion.8 = f32[227,512]{0,1:T(8,128)S(1)} fusion(bf16[16,227,512]{1,0,2:T(8,128)(2,1)} %all-to-all-done), kind=kLoop, calls=%fused_computation.13 | loop fusion | flops 3602944 | bytes 4184064 | tf_op jit(solution)/shard_map/vmap()/reduce_sum | solution.py:40
  108.3 6.6 %subtract_convert_fusion = bf16[4,256,227,8]{2,3,0,1:T(8,128)(2,1)} fusion(f32[4,256,227,8]{2,3,0,1:T(8,128)} %bitcast.130, f32[4,227,8]{1,2,0:T(8,128)S(1)} %get-tuple-element.15), kind=kLoop, calls=%fused_computation.2 | loop fusion | flops 3719168 | bytes 11186560 | tf_op jit(solution)/shard_map/vmap()/convert_element_type | solution.py:41
  115.0 35.4 %all-to-all-done.1 = bf16[16,16,1,8704]{3,1,2,0:T(8,128)(2,1)} async-done(((bf16[16,16,1,8704]{3,1,2,0:T(8,128)(2,1)}), bf16[16,16,1,8704]{3,1,2,0:T(8,128)(2,1)}, u32[]{:S(2)}, u32[]{:S(2)}) %all-to-all-start.1) | async-done | bytes 4456480 | tf_op jit(solution)/shard_map/all_to_all | solution.py:12
  150.4 6.6 %copy.27 = bf16[256,8704]{0,1:T(8,128)(2,1)} copy(bf16[256,8704]{1,0:T(8,128)(2,1)} %bitcast.5) | data formatting | bytes 8912896 | tf_op jit(solution)/shard_map/squeeze;reshape | solution.py:99
  157.0 9.5 %gather_fusion = bf16[2048,256]{1,0:T(8,128)(2,1)S(1)} fusion(bf16[256,8704]{0,1:T(8,128)(2,1)} %copy.27, s32[2048]{0:T(1024)S(1)} %broadcast_clamp_fusion.1), kind=kCustom, calls=%fused_computation | custom fusion | bytes 2105344 | tf_op jit(solution)/shard_map/jit(_take)/gather | solution.py:99
  168.3 1.5 multiply_reduce_fusion
  171.3 1.2 fusion.31
  179.5 1.4 fusion.14
  192.0 5.6 %fusion = bf16[256,227,4,8]{0,1,3,2:T(8,128)(2,1)} fusion(f32[227,4,8]{0,2,1:T(8,128)S(1)} %get-tuple-element.16, bf16[4,256,227,8]{2,3,0,1:T(8,128)(2,1)S(1)} %copy-done, f32[4,256,256]{2,1,0:T(8,128)S(1)} %convolution_divide_fusion, f32[4,256]{1,0:T(4,128)S(1)} %bitcast.145), kind=kOutput, calls=%fused_computation.4 | convolution fusion | flops 956612608 | bytes 8520064 | tf_op jit(solution)/shard_map/vmap(jvc,jk->kvc)/dot_general | solution.py:71
  197.7 7.8 %copy.33 = bf16[256,227,32]{1,2,0:T(8,128)(2,1)} copy(bf16[256,227,32]{0,1,2:T(8,128)(2,1)} %bitcast.135) | data formatting | bytes 7438336 | tf_op jit(solution)/shard_map/reshape | solution.py:108
  205.5 53.6 %all_to_all.32 = bf16[256,227,32]{1,2,0:T(8,128)(2,1)S(1)} all-to-all(bf16[256,227,32]{1,2,0:T(8,128)(2,1)} %copy.33), channel_id=1, replica_groups=mesh['mem'=16,'reg'=16] {'mem'}, dimensions={0} | all-to-all | bytes 7438336 | tf_op jit(solution)/shard_map/all_to_all | solution.py:109
  259.1 2.4 copy.34
  261.5 7.3 %copy.35 = bf16[16,227,512]{2,0,1:T(8,128)(2,1)} copy(bf16[16,227,512]{1,2,0:T(8,128)(2,1)} %bitcast.133) | data formatting | bytes 7438336 | tf_op jit(solution)/shard_map/all_to_all | solution.py:109
  (66 shorter events, 22.5 us)
Async XLA Ops:
  8.2 7.3 %copy-start.1 = (bf16[16,1,8192]{2,0,1:T(8,128)(2,1)S(1)}, bf16[16,1,8192]{2,0,1:T(8,128)(2,1)}, u32[]{:S(2)}) copy-start(bf16[16,1,8192]{2,0,1:T(8,128)(2,1)} %param.7) | copy-start | bytes 786436
  8.2 7.8 %copy-start.3 = (f32[1,8192]{1,0:T(1,128)S(1)}, f32[1,8192]{1,0:T(1,128)}, u32[]{:S(2)}) copy-start(f32[1,8192]{1,0:T(1,128)} %param.8) | copy-start | bytes 98308
  8.2 7.8 %copy-start.4 = (f32[1,8192]{1,0:T(1,128)S(1)}, f32[1,8192]{1,0:T(1,128)}, u32[]{:S(2)}) copy-start(f32[1,8192]{1,0:T(1,128)} %param.9) | copy-start | bytes 98308
  8.2 10.7 %copy-start.2 = (s32[1,1,4,512]{3,2,1,0:T(4,128)S(1)}, s32[1,1,4,512]{3,2,1,0:T(4,128)}, u32[]{:S(2)}) copy-start(s32[1,1,4,512]{3,2,1,0:T(4,128)} %param.10) | copy-start | bytes 24580
  8.2 70.5 %all-to-all-start = ((bf16[16,227,512]{1,0,2:T(8,128)(2,1)}), bf16[16,227,512]{1,0,2:T(8,128)(2,1)}, u32[]{:S(2)}, u32[]{:S(2)}) async-start(bf16[16,227,512]{1,0,2:T(8,128)(2,1)} %copy.25), calls=%async_computation | async-start | bytes 8388608 | tf_op jit(solution)/shard_map/all_to_all | solution.py:88
  15.5 3.4 %collective-permute-start.1 = (bf16[16,1,256]{2,0,1:T(8,128)(2,1)S(1)}, bf16[16,1,256]{2,0,1:T(8,128)(2,1)S(1)}, u32[]{:S(2)}, u32[]{:S(2)}) collective-permute-start(bf16[16,1,256]{2,0,1:T(8,128)(2,1)S(1)} %get-tuple-element.8), channel_id=1, source_target_pairs={{1,0},{2,1},{3,2},{4,3},{5,4},{6,5},{7,6},{8,7},{9,8},{10,9},{11,1... | collective-permute-start | bytes 24584 | tf_op jit(solution)/shard_map/ppermute | solution.py:28
  15.5 3.4 %collective-permute-start = (bf16[16,1,256]{2,0,1:T(8,128)(2,1)S(1)}, bf16[16,1,256]{2,0,1:T(8,128)(2,1)S(1)}, u32[]{:S(2)}, u32[]{:S(2)}) collective-permute-start(bf16[16,1,256]{2,0,1:T(8,128)(2,1)S(1)} %get-tuple-element.7), channel_id=1, source_target_pairs={{0,1},{1,2},{2,3},{3,4},{4,5},{5,6},{6,7},{7,8},{8,9},{9,10},{10,1... | collective-permute-start | bytes 24584 | tf_op jit(solution)/shard_map/ppermute | solution.py:26
  16.1 70.0 %collective-permute-start.3 = (bf16[2,1,256]{2,0,1:T(2,128)(2,1)S(1)}, bf16[2,1,256]{2,0,1:T(2,128)(2,1)S(1)}, u32[]{:S(2)}, u32[]{:S(2)}) collective-permute-start(bf16[2,1,256]{2,0,1:T(2,128)(2,1)S(1)} %get-tuple-element.10), channel_id=1, source_target_pairs={{1,0},{2,1},{3,2},{4,3},{5,4},{6,5},{7,6},{8,7},{9,8},{10,9},{11,1... | collective-permute-start | bytes 3080 | tf_op jit(solution)/shard_map/ppermute | solution.py:28
  17.4 68.7 %collective-permute-start.2 = (bf16[2,1,256]{2,0,1:T(2,128)(2,1)S(1)}, bf16[2,1,256]{2,0,1:T(2,128)(2,1)S(1)}, u32[]{:S(2)}, u32[]{:S(2)}) collective-permute-start(bf16[2,1,256]{2,0,1:T(2,128)(2,1)S(1)} %get-tuple-element.9), channel_id=1, source_target_pairs={{0,1},{1,2},{2,3},{3,4},{4,5},{5,6},{6,7},{7,8},{8,9},{9,10},{10,1... | collective-permute-start | bytes 3080 | tf_op jit(solution)/shard_map/ppermute | solution.py:26
  81.2 69.2 %all-to-all-start.1 = ((bf16[16,16,1,8704]{3,1,2,0:T(8,128)(2,1)}), bf16[16,16,1,8704]{3,1,2,0:T(8,128)(2,1)}, u32[]{:S(2)}, u32[]{:S(2)}) async-start(bf16[16,16,1,8704]{3,1,2,0:T(8,128)(2,1)} %stack.10), calls=%async_computation.1 | async-start | bytes 8912896 | tf_op jit(solution)/shard_map/all_to_all | solution.py:12
  166.5 1.8 copy-start.5
  187.7 4.4 %copy-start = (bf16[4,256,227,8]{2,3,0,1:T(8,128)(2,1)S(1)}, bf16[4,256,227,8]{2,3,0,1:T(8,128)(2,1)}, u32[]{:S(2)}) copy-start(bf16[4,256,227,8]{2,3,0,1:T(8,128)(2,1)} %subtract_convert_fusion) | copy-start | bytes 11157508
